TPU v7x, 32 devices: a whole 2x2x4 slice. The times are simulated.
32 devices in a mesh: dp: 8 (over y, x, core), seq: 4 (over z).
Axes of the slice: x: 2, y: 2, z: 4, core: 2. Of those that a mesh axis runs over, the one named last changes fastest.
Arguments:
- block_input: bfloat16 [8, 1024, 2048], P('dp', 'seq'), may hold values from -6 to 6
- norm_gain: float32 [2048], replicated, may hold values from 0.5 to 1.5
- in_proj: bfloat16 [2048, 2816], P(('dp', 'seq')), may hold values from -0.125 to 0.125
- gate_proj: bfloat16 [2048, 2816], P(('dp', 'seq')), may hold values from -0.125 to 0.125
- conv_kernel: float32 [4, 2816], replicated, may hold values from -3 to 3
- conv_bias: float32 [2816], replicated, may hold values from -3 to 3
- recur_weight: bfloat16 [16, 176, 176], replicated, may hold values from -0.4375 to 0.4375
- recur_bias: float32 [2816], replicated, may hold values from -3 to 3
- input_weight: bfloat16 [16, 176, 176], replicated, may hold values from -0.4375 to 0.4375
- input_bias: float32 [2816], replicated, may hold values from -3 to 3
- decay_param: float32 [2816], replicated, may hold values from 5 to 10
- out_proj: bfloat16 [2816, 2048], P(('dp', 'seq')), may hold values from -0.3125 to 0.3125
- mlp_gain: float32 [2048], replicated, may hold values from 0.5 to 1.5
- mlp_gate: bfloat16 [2048, 6144], P(('dp', 'seq')), may hold values from -0.125 to 0.125
- mlp_up: bfloat16 [2048, 6144], P(('dp', 'seq')), may hold values from -0.125 to 0.125
- mlp_down: bfloat16 [6144, 2048], P(('dp', 'seq')), may hold values from -0.109375 to 0.109375
- out_grad: bfloat16 [8, 1024, 2048], P('dp', 'seq'), may hold values from -6 to 6
Outputs:
- block_output: bfloat16 [8, 1024, 2048], P('dp', 'seq')
- input_grad: float32 [8, 1024, 2048], P('dp', 'seq')
- grad_norm_gain: float32 [2048], replicated
- grad_in_proj: float32 [2048, 2816], P('seq', 'dp')
- grad_gate_proj: float32 [2048, 2816], P('seq', 'dp')
- grad_conv_kernel: float32 [4, 2816], replicated
- grad_conv_bias: float32 [2816], replicated
- grad_recur_weight: float32 [16, 176, 176], replicated
- grad_recur_bias: float32 [2816], replicated
- grad_input_weight: float32 [16, 176, 176], replicated
- grad_input_bias: float32 [2816], replicated
- grad_decay_param: float32 [2816], replicated
- grad_out_proj: float32 [2816, 2048], P('seq', 'dp')
- grad_mlp_gain: float32 [2048], replicated
- grad_mlp_gate: float32 [2048, 6144], P('seq', 'dp')
- grad_mlp_up: float32 [2048, 6144], P('seq', 'dp')
- grad_mlp_down: float32 [6144, 2048], P('seq', 'dp')
All inputs are finite; a program needn't handle non-finite values.
Results may differ from a plain program's by a relative error of at most 0.015.
Values may be sent and summed in bfloat16 or wider, within the bound.
No kernel may reach another device: no remote copies, remote signals or barrier semaphores. Data moves between devices by JAX's collectives and lax.ppermute only.
A program may use at most 640 MiB of HBM per device.

v0:
```python
import jax
import jax.numpy as jnp
from jax import lax
from jax.sharding import PartitionSpec as P

EPSILON = 1e-06


def from_behind(value, axis, steps):
    count = lax.axis_size(axis)
    initial, last = (max(0, -steps), min(count, count - steps))
    return lax.ppermute(value, axis, [(source, source + steps) for source in range(initial, last)])


def scaled_norm(values, gain_vec):
    return (
        values * lax.rsqrt(jnp.mean(values * values, axis=-1, keepdims=True) + EPSILON) * gain_vec
    )


def recurrence_gates(recur_pre, input_pre, conv_out, decay_param):
    recur_gate = jax.nn.sigmoid(recur_pre)
    input_gate = jax.nn.sigmoid(input_pre)
    log_rate = -8.0 * recur_gate * jax.nn.softplus(-decay_param)
    decay_rate = jnp.exp(log_rate)
    driven = jnp.sqrt(-jnp.expm1(2.0 * log_rate)) * input_gate * conv_out
    return (decay_rate, driven)


def gated_product(gate_values, up_values):
    return jax.nn.gelu(gate_values) * up_values


def compose(earlier, later):
    return (earlier[0] * later[0], earlier[1] * later[0] + later[1])


def matmul_back(grad_rows, weight_full):
    return lax.dot_general(
        grad_rows, weight_full, (((1,), (1,)), ((), ())), preferred_element_type=jnp.float32
    )


def reduce_weight_grad(left_side, right_side):
    inner_sum = lax.psum_scatter(
        lax.dot_general(
            left_side, right_side, (((0,), (0,)), ((), ())), preferred_element_type=jnp.float32
        ).astype(jnp.bfloat16),
        "seq",
        scatter_dimension=0,
        tiled=True,
    )
    return lax.psum_scatter(inner_sum, "dp", scatter_dimension=1, tiled=True).astype(jnp.float32)


def local(
    block_input,
    norm_gain,
    in_proj,
    gate_proj,
    conv_kernel,
    conv_bias,
    recur_weight,
    recur_bias,
    input_weight,
    input_bias,
    decay_param,
    out_proj,
    mlp_gain,
    mlp_gate,
    mlp_up,
    mlp_down,
    out_grad,
):
    seq_count = lax.axis_size("seq")
    model_width = block_input.shape[2]
    tokens = block_input.reshape(-1, model_width).astype(jnp.float32)
    length = tokens.shape[0]
    head_count = recur_weight.shape[0]
    head_size = recur_weight.shape[1]
    tap_count = conv_kernel.shape[0]
    conv_lag = tap_count - 1
    fwd_recur = (
        lax.all_gather(in_proj, ("dp", "seq"), axis=0, tiled=True),
        lax.all_gather(gate_proj, ("dp", "seq"), axis=0, tiled=True),
        lax.all_gather(out_proj, ("dp", "seq"), axis=0, tiled=True),
    )
    normed = scaled_norm(tokens, norm_gain).astype(jnp.bfloat16)
    branch = jnp.dot(normed, fwd_recur[0], preferred_element_type=jnp.float32)
    gate_pre = jnp.dot(normed, fwd_recur[1], preferred_element_type=jnp.float32)
    gate_act = jax.nn.gelu(gate_pre)
    recur_width = branch.shape[1]
    prior_rows = from_behind(branch[length - conv_lag :], "seq", 1)
    padded = jnp.concatenate([prior_rows, branch], axis=0)
    conv_out = jnp.zeros((length, recur_width), jnp.float32) + conv_bias
    for tap_index in range(tap_count):
        begin = conv_lag - tap_index
        conv_out = conv_out + conv_kernel[tap_index] * padded[begin : begin + length]
    heads_in = conv_out.astype(jnp.bfloat16).reshape(length, head_count, head_size)
    recur_pre = (
        jnp.einsum(
            "thi,hij->thj", heads_in, recur_weight, preferred_element_type=jnp.float32
        ).reshape(length, recur_width)
        + recur_bias
    )
    input_pre = (
        jnp.einsum(
            "thi,hij->thj", heads_in, input_weight, preferred_element_type=jnp.float32
        ).reshape(length, recur_width)
        + input_bias
    )
    decay_rate, driven = recurrence_gates(recur_pre, input_pre, conv_out, decay_param)
    decay_run, local_states = lax.associative_scan(compose, (decay_rate, driven), axis=0)
    zero_row = jnp.zeros((recur_width,), jnp.float32)
    carried = zero_row
    for repeat in range(seq_count - 1):
        carried = from_behind(decay_run[length - 1] * carried + local_states[length - 1], "seq", 1)
    states = local_states + decay_run * carried
    mixed_out = (states * gate_act).astype(jnp.bfloat16)
    residual = tokens + jnp.dot(mixed_out, fwd_recur[2], preferred_element_type=jnp.float32)
    fwd_ffn = (
        lax.all_gather(mlp_gate, ("dp", "seq"), axis=0, tiled=True),
        lax.all_gather(mlp_up, ("dp", "seq"), axis=0, tiled=True),
        lax.all_gather(mlp_down, ("dp", "seq"), axis=0, tiled=True),
    )
    normed_two = scaled_norm(residual, mlp_gain).astype(jnp.bfloat16)
    ffn_gate = jnp.dot(normed_two, fwd_ffn[0], preferred_element_type=jnp.float32)
    ffn_up = jnp.dot(normed_two, fwd_ffn[1], preferred_element_type=jnp.float32)
    hidden = gated_product(ffn_gate, ffn_up).astype(jnp.bfloat16)
    result = residual + jnp.dot(hidden, fwd_ffn[2], preferred_element_type=jnp.float32)
    block_output = result.astype(jnp.bfloat16).reshape(block_input.shape)
    back_recur = (
        lax.all_gather(in_proj, ("dp", "seq"), axis=0, tiled=True),
        lax.all_gather(gate_proj, ("dp", "seq"), axis=0, tiled=True),
        lax.all_gather(out_proj, ("dp", "seq"), axis=0, tiled=True),
    )
    back_ffn = (
        lax.all_gather(mlp_gate, ("dp", "seq"), axis=0, tiled=True),
        lax.all_gather(mlp_up, ("dp", "seq"), axis=0, tiled=True),
        lax.all_gather(mlp_down, ("dp", "seq"), axis=0, tiled=True),
    )
    grad_low = out_grad.reshape(length, model_width)
    grad_top = grad_low.astype(jnp.float32)
    grad_down_w = reduce_weight_grad(hidden, grad_low)
    grad_hidden = matmul_back(grad_low, back_ffn[2])
    unused, pull_ffn = jax.vjp(gated_product, ffn_gate, ffn_up)
    grad_ffn_gate, grad_ffn_up = pull_ffn(grad_hidden)
    grad_ffn_gate = grad_ffn_gate.astype(jnp.bfloat16)
    grad_ffn_up = grad_ffn_up.astype(jnp.bfloat16)
    grad_mgate_w = reduce_weight_grad(normed_two, grad_ffn_gate)
    grad_mup_w = reduce_weight_grad(normed_two, grad_ffn_up)
    grad_normed_two = matmul_back(grad_ffn_gate, back_ffn[0]) + matmul_back(
        grad_ffn_up, back_ffn[1]
    )
    unused, pull_norm_two = jax.vjp(scaled_norm, residual, mlp_gain)
    grad_resid_part, mlp_gain_term = pull_norm_two(grad_normed_two)
    grad_residual = grad_resid_part + grad_top
    grad_rec = grad_residual.astype(jnp.bfloat16)
    grad_out_w = reduce_weight_grad(mixed_out, grad_rec)
    grad_mixed = matmul_back(grad_rec, back_recur[2])
    grad_states = grad_mixed * gate_act
    unused, pull_gelu = jax.vjp(jax.nn.gelu, gate_pre)
    grad_gate_pre = pull_gelu(grad_mixed * states)[0].astype(jnp.bfloat16)
    next_decay = jnp.concatenate([decay_rate[1:], jnp.ones((1, recur_width), jnp.float32)], axis=0)
    decay_tail, local_grads = lax.associative_scan(
        compose, (next_decay, grad_states), reverse=True, axis=0
    )
    total_decay = decay_rate[0] * decay_tail[0]
    first_grad = decay_rate[0] * local_grads[0]
    later_grad = zero_row
    for repeat in range(seq_count - 1):
        later_grad = from_behind(total_decay * later_grad + first_grad, "seq", -1)
    state_grads = local_grads + decay_tail * later_grad
    prior_states = jnp.concatenate([carried[None], states[: length - 1]], axis=0)
    unused, pull_gates = jax.vjp(recurrence_gates, recur_pre, input_pre, conv_out, decay_param)
    grad_recur_pre, grad_input_pre, grad_conv, decay_term = pull_gates(
        (state_grads * prior_states, state_grads)
    )
    grad_recur_low = grad_recur_pre.astype(jnp.bfloat16).reshape(length, head_count, head_size)
    grad_input_low = grad_input_pre.astype(jnp.bfloat16).reshape(length, head_count, head_size)
    recur_w_term = jnp.einsum(
        "thi,thj->hij", heads_in, grad_recur_low, preferred_element_type=jnp.float32
    )
    input_w_term = jnp.einsum(
        "thi,thj->hij", heads_in, grad_input_low, preferred_element_type=jnp.float32
    )
    recur_b_term = jnp.sum(grad_recur_low.astype(jnp.float32), axis=0).reshape(recur_width)
    input_b_term = jnp.sum(grad_input_low.astype(jnp.float32), axis=0).reshape(recur_width)
    grad_conv = grad_conv + jnp.einsum(
        "thj,hij->thi", grad_recur_low, recur_weight, preferred_element_type=jnp.float32
    ).reshape(length, recur_width)
    grad_conv = grad_conv + jnp.einsum(
        "thj,hij->thi", grad_input_low, input_weight, preferred_element_type=jnp.float32
    ).reshape(length, recur_width)
    later_rows = from_behind(grad_conv[:conv_lag].astype(jnp.bfloat16), "seq", -1).astype(
        jnp.float32
    )
    grad_padded = jnp.concatenate([grad_conv, later_rows], axis=0)
    grad_branch = jnp.zeros((length, recur_width), jnp.float32)
    kernel_rows = []
    for tap_index in range(tap_count):
        grad_branch = (
            grad_branch + conv_kernel[tap_index] * grad_padded[tap_index : tap_index + length]
        )
        begin = conv_lag - tap_index
        kernel_rows.append(jnp.sum(grad_conv * padded[begin : begin + length], axis=0))
    kernel_term = jnp.stack(kernel_rows, axis=0)
    bias_term = jnp.sum(grad_conv, axis=0)
    grad_branch = grad_branch.astype(jnp.bfloat16)
    grad_in_w = reduce_weight_grad(normed, grad_branch)
    grad_gate_w = reduce_weight_grad(normed, grad_gate_pre)
    grad_normed = matmul_back(grad_branch, back_recur[0]) + matmul_back(
        grad_gate_pre, back_recur[1]
    )
    unused, pull_norm = jax.vjp(scaled_norm, tokens, norm_gain)
    grad_tokens, norm_gain_term = pull_norm(grad_normed)
    input_grad = (grad_tokens + grad_residual).reshape(block_input.shape)
    summed = lax.psum(
        (
            norm_gain_term,
            kernel_term,
            bias_term,
            recur_w_term,
            recur_b_term,
            input_w_term,
            input_b_term,
            decay_term,
            mlp_gain_term,
        ),
        ("dp", "seq"),
    )
    return (
        block_output,
        input_grad,
        summed[0],
        grad_in_w,
        grad_gate_w,
        summed[1],
        summed[2],
        summed[3],
        summed[4],
        summed[5],
        summed[6],
        summed[7],
        grad_out_w,
        summed[8],
        grad_mgate_w,
        grad_mup_w,
        grad_down_w,
    )


def solution(mesh):
    return jax.shard_map(
        local,
        mesh=mesh,
        in_specs=(
            P("dp", "seq", None),
            P(),
            P(("dp", "seq"), None),
            P(("dp", "seq"), None),
            P(),
            P(),
            P(),
            P(),
            P(),
            P(),
            P(),
            P(("dp", "seq"), None),
            P(),
            P(("dp", "seq"), None),
            P(("dp", "seq"), None),
            P(("dp", "seq"), None),
            P("dp", "seq", None),
        ),
        out_specs=(
            P("dp", "seq", None),
            P("dp", "seq", None),
            P(),
            P("seq", "dp"),
            P("seq", "dp"),
            P(),
            P(),
            P(),
            P(),
            P(),
            P(),
            P(),
            P("seq", "dp"),
            P(),
            P("seq", "dp"),
            P("seq", "dp"),
            P("seq", "dp"),
        ),
        check_vma=False,
    )
```

profile of v0, /device:TPU:0, one launch (start us, length us, event | category | flops | bytes accessed | tf_op | source)
XLA Modules:
  0.0 3378.2 jit_solution(6021144712687071717)
XLA Ops:
  11.6 93.3 %all-gather.7.cloned.1.call-done = bf16[2048,2816]{1,0:T(8,128)(2,1)} async-done(((bf16[64,2816]{1,0:T(8,128)(2,1)}), bf16[2048,2816]{1,0:T(8,128)(2,1)}) %all-gather.7.cloned.1.call-update) | async-done | bytes 11534352 | tf_op jit(solution)/shard_map/all_gather | solution.py:84
  104.9 6.3 fusion.83
  136.8 9.1 multiply_exponential_fusion
  157.2 5.8 slice.557
  163.0 5.7 slice.559
  250.9 6.2 slice.613
  257.1 6.0 slice.614
  324.3 9.6 pad.228
  333.9 9.4 pad.229
  345.9 9.4 pad.212
  355.3 9.3 pad.213
  384.0 13.3 multiply_convert_fusion.2
  397.3 6.6 multiply_reduce_fusion.7
  405.5 40.2 %all-gather.13.cloned.1.call-done = bf16[2048,6144]{1,0:T(8,128)(2,1)} async-done(((bf16[64,6144]{1,0:T(8,128)(2,1)}), bf16[2048,6144]{1,0:T(8,128)(2,1)}) %all-gather.13.cloned.1.call-update) | async-done | bytes 25165840 | tf_op jit(solution)/shard_map/all_gather | solution.py:122
  445.7 14.2 fusion.108
  460.0 141.4 %all-gather.15.cloned.1.call-done = bf16[2048,6144]{1,0:T(8,128)(2,1)} async-done(((bf16[64,6144]{1,0:T(8,128)(2,1)}), bf16[2048,6144]{1,0:T(8,128)(2,1)}) %all-gather.15.cloned.1.call-update) | async-done | bytes 25165840 | tf_op jit(solution)/shard_map/all_gather | solution.py:123
  601.3 14.4 fusion.109
  615.7 141.2 %all-gather.17.cloned.1.call-done = bf16[6144,2048]{1,0:T(8,128)(2,1)} async-done(((bf16[192,2048]{1,0:T(8,128)(2,1)}), bf16[6144,2048]{1,0:T(8,128)(2,1)}) %all-gather.17.cloned.1.call-update) | async-done | bytes 25165840 | tf_op jit(solution)/shard_map/all_gather | solution.py:124
  756.9 22.1 multiply_convert_fusion
  779.0 13.5 fusion.110
  792.6 15.7 multiply_reduce_fusion.5
  811.6 12.8 fusion.45
  824.4 7.5 convolution_convert_fusion.3
  835.7 5.8 slice.636
  852.9 11.9 slice.637
  864.7 11.9 slice.643
  876.6 12.0 slice.695
  888.6 5.7 slice.633
  894.2 5.7 slice.638
  899.9 11.9 slice.634
  911.8 11.9 slice.639
  950.3 9.5 convolution_convert_fusion.5
  1016.3 5.7 slice.696
  1068.7 9.5 pad.261
  1091.5 9.4 pad.245
  1100.9 12.0 slice.697
  1119.5 9.4 pad.244
  1131.4 9.6 pad.260
  1143.5 8.1 collective-permute-done.4
  1152.8 7.1 collective-permute-done.5
  1168.2 23.0 rev.9
  1191.1 22.7 rev.8
  1213.9 8.5 multiply_reduce_fusion
  1223.2 5.7 convert_reduce_fusion.1
  1248.1 12.1 multiply_reduce_fusion.3
  1269.5 6.2 convolution_convert_fusion.4
  1276.9 13.7 convolution_convert_fusion.2
  1290.7 13.8 convolution_convert_fusion.1
  1305.8 14.0 convolution_convert_fusion
  1325.1 144.4 %reduce-scatter.17.cloned.1.call-done = bf16[512,2816]{1,0:T(8,128)(2,1)} async-done(((bf16[2048,2816]{1,0:T(8,128)(2,1)}), bf16[512,2816]{1,0:T(8,128)(2,1)}) %reduce-scatter.17.cloned.1.call-update) | async-done | bytes 2883600 | tf_op jit(solution)/shard_map/reduce_scatter | solution.py:45
  1474.1 413.1 %reduce-scatter.25.cloned.1.call-done = bf16[512,6144]{1,0:T(8,128)(2,1)} async-done(((bf16[2048,6144]{1,0:T(8,128)(2,1)}), bf16[512,6144]{1,0:T(8,128)(2,1)}) %reduce-scatter.25.cloned.1.call-update) | async-done | bytes 6291472 | tf_op jit(solution)/shard_map/reduce_scatter | solution.py:45
  1887.2 418.7 %reduce-scatter.29.cloned.1.call-done = bf16[512,6144]{1,0:T(8,128)(2,1)} async-done(((bf16[2048,6144]{1,0:T(8,128)(2,1)}), bf16[512,6144]{1,0:T(8,128)(2,1)}) %reduce-scatter.29.cloned.1.call-update) | async-done | bytes 6291472 | tf_op jit(solution)/shard_map/reduce_scatter | solution.py:45
  2306.0 418.4 %reduce-scatter.33.cloned.1.call-done = bf16[1536,2048]{1,0:T(8,128)(2,1)} async-done(((bf16[6144,2048]{1,0:T(8,128)(2,1)}), bf16[1536,2048]{1,0:T(8,128)(2,1)}) %reduce-scatter.33.cloned.1.call-update) | async-done | bytes 6291472 | tf_op jit(solution)/shard_map/reduce_scatter | solution.py:45
  2724.5 6.6 fusion.111
  2734.0 10.0 fusion.37
  2748.2 14.7 fusion.35
  2764.8 10.6 reduce-scatter.39.cloned.1.call-done
  2777.7 45.9 %reduce-scatter.23.cloned.1.call-done = bf16[704,256]{1,0:T(8,128)(2,1)} async-done(((bf16[704,2048]{1,0:T(8,128)(2,1)}), bf16[704,256]{1,0:T(8,128)(2,1)}) %reduce-scatter.23.cloned.1.call-update) | async-done | bytes 360464 | tf_op jit(solution)/shard_map/reduce_scatter | solution.py:53
  2825.5 47.2 %reduce-scatter.37.cloned.1.call-done = bf16[352,512]{1,0:T(8,128)(2,1)} async-done(((bf16[2816,512]{1,0:T(8,128)(2,1)}), bf16[352,512]{1,0:T(8,128)(2,1)}) %reduce-scatter.37.cloned.1.call-update) | async-done | bytes 360464
  2875.0 62.7 %reduce-scatter.27.cloned.1.call-done = bf16[512,768]{1,0:T(8,128)(2,1)} async-done(((bf16[512,6144]{1,0:T(8,128)(2,1)}), bf16[512,768]{1,0:T(8,128)(2,1)}) %reduce-scatter.27.cloned.1.call-update) | async-done | bytes 786448 | tf_op jit(solution)/shard_map/reduce_scatter | solution.py:53
  2940.1 63.0 %reduce-scatter.31.cloned.1.call-done = bf16[512,768]{1,0:T(8,128)(2,1)} async-done(((bf16[512,6144]{1,0:T(8,128)(2,1)}), bf16[512,768]{1,0:T(8,128)(2,1)}) %reduce-scatter.31.cloned.1.call-update) | async-done | bytes 786448 | tf_op jit(solution)/shard_map/reduce_scatter | solution.py:53
  3005.5 62.6 %reduce-scatter.35.cloned.1.call-done = bf16[1536,256]{1,0:T(8,128)(2,1)} async-done(((bf16[1536,2048]{1,0:T(8,128)(2,1)}), bf16[1536,256]{1,0:T(8,128)(2,1)}) %reduce-scatter.35.cloned.1.call-update) | async-done | bytes 786448 | tf_op jit(solution)/shard_map/reduce_scatter | solution.py:53
  3070.5 130.0 %all-reduce.71.cloned.1.call-done = (f32[2048]{0:T(1024)}, f32[4,2816]{1,0:T(4,128)}, f32[2816]{0:T(1024)}, f32[2816]{0:T(1024)}, f32[2816]{0:T(1024)}, /*index=5*/f32[2816]{0:T(1024)}, f32[2048]{0:T(1024)}) async-done(((f32[2048]{0:T(1024)}, f32[4,2816]{1,0:T(4,128)}, f32[2816]{0:T(1024)}, f32[2816]{0:T(1024)}, f32[2816]{0:T(1024)}, /*index=5*/f32[2816]{0:T(1024)}, f32[2048]{0:T(1024)}), (f32[2048]{0:T(1024)}, ...) | async-done | bytes 106512 | tf_op jit(solution)/shard_map/psum | solution.py:218
  3200.5 158.8 %all-reduce.73.cloned.1.call-done = (f32[16,176,176]{2,1,0:T(8,128)}, f32[16,176,176]{2,1,0:T(8,128)}) async-done(((f32[16,176,176]{2,1,0:T(8,128)}, f32[16,176,176]{2,1,0:T(8,128)}), (f32[16,176,176]{2,1,0:T(8,128)}, f32[16,176,176]{2,1,0:T(8,128)})) %all-reduce.73.cloned.1.call-update) | async-done | bytes 3964944 | tf_op jit(solution)/shard_map/psum | solution.py:218
  (586 shorter events, 465.5 us)
Async XLA Ops:
  7.2 115.0 %copy-start = (bf16[16,176,176]{2,1,0:T(8,128)(2,1)S(1)}, bf16[16,176,176]{2,1,0:T(8,128)(2,1)}, u32[]{:S(2)}) copy-start(bf16[16,176,176]{2,1,0:T(8,128)(2,1)} %param.23) | copy-start | bytes 2973700
  7.2 97.7 %copy-start.41 = (f32[2048]{0:T(1024)S(1)}, f32[2048]{0:T(1024)}, u32[]{:S(2)}) copy-start(f32[2048]{0:T(1024)} %param.18) | copy-start | bytes 24580
  7.2 97.7 %all-gather.7.cloned.1.call-start = ((), (), s32[]{:S(2)}) async-start(), calls=%async_computation.12 | async-start | bytes 11894784 | tf_op jit(solution)/shard_map/all_gather | solution.py:84
  8.0 374.6 %all-gather.9.cloned.1.call-start = ((), (), s32[]{:S(2)}) async-start(), calls=%async_computation.13 | async-start | bytes 11894784 | tf_op jit(solution)/shard_map/all_gather | solution.py:85
  8.7 388.6 %all-gather.11.cloned.1.call-start = ((), (), s32[]{:S(2)}) async-start(), calls=%async_computation.14 | async-start | bytes 11894784 | tf_op jit(solution)/shard_map/all_gather | solution.py:86
  9.5 436.3 %all-gather.13.cloned.1.call-start = ((), (), s32[]{:S(2)}) async-start(), calls=%async_computation.15 | async-start | bytes 25952256 | tf_op jit(solution)/shard_map/all_gather | solution.py:122
  10.0 591.3 %all-gather.15.cloned.1.call-start = ((), (), s32[]{:S(2)}) async-start(), calls=%async_computation.16 | async-start | bytes 25952256 | tf_op jit(solution)/shard_map/all_gather | solution.py:123
  10.6 746.3 %all-gather.17.cloned.1.call-start = ((), (), s32[]{:S(2)}) async-start(), calls=%async_computation.17 | async-start | bytes 25952256 | tf_op jit(solution)/shard_map/all_gather | solution.py:124
  11.2 1308.7 %reduce-scatter.19.cloned.1.call-start = ((), (), s32[]{:S(2)}) async-start(), calls=%async_computation.19 | async-start | bytes 14417920 | tf_op jit(solution)/shard_map/reduce_scatter | solution.py:45
  11.5 99.7 %copy-start.112 = (f32[256]{0:T(256)}, f32[256]{0:T(256)S(1)}, u32[]{:S(2)}) copy-start(f32[256]{0:T(256)S(1)} %fusion.41) | copy-start | bytes 3076
  11.6 125.2 %copy-start.44 = (f32[2816]{0:T(1024)}, f32[2816]{0:T(1024)S(1)}, u32[]{:S(2)}) copy-start(f32[2816]{0:T(1024)S(1)} %broadcast_multiply_fusion) | copy-start | bytes 33796
  11.6 102.9 %copy-start.97 = (f32[4,2816]{1,0:T(4,128)S(1)}, f32[4,2816]{1,0:T(4,128)}, u32[]{:S(2)}) copy-start(f32[4,2816]{1,0:T(4,128)} %param.21) | copy-start | bytes 135172
  11.6 105.1 %copy-start.108 = (f32[2816]{0:T(1024)S(1)}, f32[2816]{0:T(1024)}, u32[]{:S(2)}) copy-start(f32[2816]{0:T(1024)} %param.22) | copy-start | bytes 33796
  111.3 5.5 collective-permute-start
  250.9 15.2 copy-start.66
  250.9 15.2 copy-start.67
  250.9 15.2 copy-start.68
  250.9 15.2 copy-start.69
  250.9 15.3 copy-start.46
  250.9 15.7 copy-start.54
  250.9 15.7 copy-start.55
  366.6 5.7 collective-permute-start.1
  372.3 5.8 collective-permute-start.2
  378.2 5.8 collective-permute-start.3
  405.5 195.8 %copy-start.14 = (bf16[256,2048]{1,0:T(8,128)(2,1)}, bf16[256,2048]{1,0:T(8,128)(2,1)S(1)}, u32[]{:S(2)}) copy-start(bf16[256,2048]{1,0:T(8,128)(2,1)S(1)} %multiply_convert_fusion.3) | copy-start | bytes 3145732
  779.0 13.5 copy-start.107
  792.6 15.7 copy-start.116
  831.9 492.6 %reduce-scatter.21.cloned.1.call-start = ((), (), s32[]{:S(2)}) async-start(), calls=%async_computation.20 | async-start | bytes 14417920 | tf_op jit(solution)/shard_map/reduce_scatter | solution.py:45
  959.9 509.7 %reduce-scatter.17.cloned.1.call-start = ((), (), s32[]{:S(2)}) async-start(), calls=%async_computation.18 | async-start | bytes 14417920 | tf_op jit(solution)/shard_map/reduce_scatter | solution.py:45
  1006.2 17.4 copy-start.70
  1006.2 17.4 copy-start.71
  1006.2 17.4 copy-start.72
  1006.2 17.4 copy-start.73
  1006.2 17.5 copy-start.47
  1009.8 14.3 copy-start.56
  1009.8 14.4 copy-start.57
  1009.8 14.4 copy-start.96
  1009.8 14.5 copy-start.95
  1131.4 29.8 copy-start.75
  1142.2 9.4 collective-permute-start.4
  1151.5 8.4 collective-permute-start.5
  1159.9 54.0 %collective-permute-start.6 = (f32[2816]{0:T(1024)S(1)}, f32[2816]{0:T(1024)S(1)}, u32[]{:S(2)}, u32[]{:S(2)}) collective-permute-start(f32[2816]{0:T(1024)S(1)} %multiply_add_fusion.17), channel_id=1, source_target_pairs={{1,0},{2,1},{3,2},{5,4},{6,5},{7,6},{9,8},{10,9},{11,10},{13,12},{... | collective-permute-start | bytes 33800 | tf_op jit(solution)/shard_map/ppermute | solution.py:12
  1191.1 22.7 copy-start.45
  1191.1 22.7 copy-start.49
  1191.1 22.7 copy-start.51
  1248.1 18.5 copy-start.59
  1248.1 18.5 copy-start.61
  1248.1 18.5 copy-start.63
  1248.1 18.5 copy-start.65
  1260.3 6.3 collective-permute-start.7
  1275.7 611.4 %reduce-scatter.25.cloned.1.call-start = ((), (), s32[]{:S(2)}) async-start(), calls=%async_computation.22 | async-start | bytes 31457280 | tf_op jit(solution)/shard_map/reduce_scatter | solution.py:45
  1290.7 1015.3 %reduce-scatter.29.cloned.1.call-start = ((), (), s32[]{:S(2)}) async-start(), calls=%async_computation.24 | async-start | bytes 31457280 | tf_op jit(solution)/shard_map/reduce_scatter | solution.py:45
  1304.6 1419.8 %reduce-scatter.33.cloned.1.call-start = ((), (), s32[]{:S(2)}) async-start(), calls=%async_computation.26 | async-start | bytes 31457280 | tf_op jit(solution)/shard_map/reduce_scatter | solution.py:45
  1319.8 1455.7 %reduce-scatter.39.cloned.1.call-start = ((), (), s32[]{:S(2)}) async-start(), calls=%async_computation.29 | async-start | bytes 3244032
  1324.5 1499.2 %reduce-scatter.23.cloned.1.call-start = ((), (), s32[]{:S(2)}) async-start(), calls=%async_computation.21 | async-start | bytes 3244032 | tf_op jit(solution)/shard_map/reduce_scatter | solution.py:53
  1325.0 1547.7 %reduce-scatter.37.cloned.1.call-start = ((), (), s32[]{:S(2)}) async-start(), calls=%async_computation.28 | async-start | bytes 3244032
  1474.1 1463.7 %reduce-scatter.27.cloned.1.call-start = ((), (), s32[]{:S(2)}) async-start(), calls=%async_computation.23 | async-start | bytes 7077888 | tf_op jit(solution)/shard_map/reduce_scatter | solution.py:53
  1887.2 1115.9 %reduce-scatter.31.cloned.1.call-start = ((), (), s32[]{:S(2)}) async-start(), calls=%async_computation.25 | async-start | bytes 7077888 | tf_op jit(solution)/shard_map/reduce_scatter | solution.py:53
  2305.9 762.1 %reduce-scatter.35.cloned.1.call-start = ((), (), s32[]{:S(2)}) async-start(), calls=%async_computation.27 | async-start | bytes 7077888 | tf_op jit(solution)/shard_map/reduce_scatter | solution.py:53
  2724.4 476.1 %all-reduce.71.cloned.1.call-start = ((), (), s32[]{:S(2)}) async-start(), calls=%async_computation.30 | async-start | bytes 221184 | tf_op jit(solution)/shard_map/psum | solution.py:218
  2744.1 615.2 %all-reduce.73.cloned.1.call-start = ((), (), s32[]{:S(2)}) async-start(), calls=%async_computation.31 | async-start | bytes 11534336 | tf_op jit(solution)/shard_map/psum | solution.py:218
  2748.1 14.8 copy-start.113
  2748.1 14.8 copy-start.8
  2748.1 14.8 copy-start.40
  (81 other events, 447.3 us)
Sparse Core Ops, SparseCore 0:
  10.9 93.9 all-gather.6
  107.7 89.6 all-gather.8
  200.2 89.6 all-gather.10
  292.7 153.0 all-gather.12
  448.5 152.8 all-gather.14
  604.1 152.8 all-gather.16
  832.0 193.1 reduce-scatter.18
  1027.5 196.7 reduce-scatter.20
  1275.9 193.6 reduce-scatter.16
  1471.7 415.4 reduce-scatter.24
  1889.7 416.1 reduce-scatter.28
  2308.1 416.1 reduce-scatter.32
  2728.7 46.7 reduce-scatter.38
  2778.7 44.8 reduce-scatter.22
  2827.8 44.8 reduce-scatter.36
  2876.0 61.6 reduce-scatter.26
  2941.3 61.7 reduce-scatter.30
  3006.4 61.6 reduce-scatter.34
  3076.8 123.6 all-reduce.70
  3206.2 153.0 all-reduce.72
where the time goes:
time: 3400 us; the launch traced here: 3380 us
  waiting for transfers between devices  2420 us (71%)
  local copies, waits for them, and re-layouts  523 us (15%)
  matrix products  236 us (7%)
  other arithmetic  158 us (5%)
    reduce_scatter x6, waiting for transfers between devices, reduce_weight_grad(): lax.psum_scatter(lax.dot_general(left_side, right_side, (((0,), (0,)), ((...  1390 us
    psum x2, waiting for transfers between devices, local(): lax.psum((norm_gain_term, kernel_term, bias_term, recur_w_term, recur_b_t...  289 us
    reduce_scatter x4, waiting for transfers between devices, reduce_weight_grad(): lax.psum_scatter(inner_sum, 'dp', scatter_dimension=1, tiled=True)  234 us
    slice x57, local copies, waits for them, and re-layouts, local(): lax.associative_scan(compose, (next_decay, grad_states), reverse=True, ax...  175 us
    all_gather x1, waiting for transfers between devices, local(): lax.all_gather(mlp_up, ('dp', 'seq'), axis=0, tiled=True)  141 us
    all_gather x1, waiting for transfers between devices, local(): lax.all_gather(mlp_down, ('dp', 'seq'), axis=0, tiled=True)  141 us
    slice x52, local copies, waits for them, and re-layouts, local(): lax.associative_scan(compose, (decay_rate, driven), axis=0)  105 us
    all_gather x1, waiting for transfers between devices, local(): lax.all_gather(in_proj, ('dp', 'seq'), axis=0, tiled=True)  93.3 us
  transfers between devices with their start and end apart: 28, of which 23 were waited for; matrix products, arithmetic and copies ran while one was open for 24% of the time, Pallas kernels for 0%

commit v1 on v0

--- a/solution.py
+++ b/solution.py
@@ -216,18 +216,21 @@
     grad_tokens, norm_gain_term = pull_norm(grad_normed)
     input_grad = (grad_tokens + grad_residual).reshape(block_input.shape)
     summed = lax.psum(
-        (
-            norm_gain_term,
-            kernel_term,
-            bias_term,
-            recur_w_term,
-            recur_b_term,
-            input_w_term,
-            input_b_term,
-            decay_term,
-            mlp_gain_term,
+        lax.psum(
+            (
+                norm_gain_term,
+                kernel_term,
+                bias_term,
+                recur_w_term,
+                recur_b_term,
+                input_w_term,
+                input_b_term,
+                decay_term,
+                mlp_gain_term,
+            ),
+            "seq",
         ),
-        ("dp", "seq"),
+        "dp",
     )
     return (
         block_output,

time: 3400 us -> 3510 us (1.032)
  waiting for transfers between devices: 2420 us -> 2540 us
    psum x0 -> x2, waiting for transfers between devices: none -> 158 us  [local(): lax.psum(lax.psum((norm_gain_term, kernel_term, bias_term, recur_w_term,...]
    psum x2, waiting for transfers between devices: 289 us -> 249 us  [local(): lax.psum((norm_gain_term, kernel_term, bias_term, recur_w_term, recur_b_t...]
    unnamed x22 -> x24, waiting for transfers between devices: 62.2 us -> 82.4 us
  transfers between devices with their start and end apart: 28 -> 30, of which waited for: 23 -> 25; matrix products, arithmetic and copies ran while one was open for 24% -> 24% of each run, Pallas kernels for 0% -> 0%
where the time goes in v1:
time: 3510 us; the launch traced here: 3490 us
  waiting for transfers between devices  2540 us (72%)
  local copies, waits for them, and re-layouts  523 us (15%)
  matrix products  235 us (7%)
  other arithmetic  158 us (5%)
    reduce_scatter x6, waiting for transfers between devices, reduce_weight_grad(): lax.psum_scatter(lax.dot_general(left_side, right_side, (((0,), (0,)), ((...  1370 us
    psum x2, waiting for transfers between devices, local(): lax.psum((norm_gain_term, kernel_term, bias_term, recur_w_term, recur_b_t...  249 us
    reduce_scatter x4, waiting for transfers between devices, reduce_weight_grad(): lax.psum_scatter(inner_sum, 'dp', scatter_dimension=1, tiled=True)  235 us
    slice x57, local copies, waits for them, and re-layouts, local(): lax.associative_scan(compose, (next_decay, grad_states), reverse=True, ax...  175 us
    psum x2, waiting for transfers between devices, local(): lax.psum(lax.psum((norm_gain_term, kernel_term, bias_term, recur_w_term,...  158 us
    all_gather x1, waiting for transfers between devices, local(): lax.all_gather(mlp_up, ('dp', 'seq'), axis=0, tiled=True)  141 us
    all_gather x1, waiting for transfers between devices, local(): lax.all_gather(mlp_down, ('dp', 'seq'), axis=0, tiled=True)  141 us
    slice x52, local copies, waits for them, and re-layouts, local(): lax.associative_scan(compose, (decay_rate, driven), axis=0)  105 us
  transfers between devices with their start and end apart: 30, of which 25 were waited for; matrix products, arithmetic and copies ran while one was open for 24% of the time, Pallas kernels for 0%

profile of v1, /device:TPU:0, one launch (start us, length us, event | category | flops | bytes accessed | tf_op | source)
XLA Modules:
  0.0 3493.8 jit_solution(2600021343039006961)
XLA Ops:
  11.6 93.3 %all-gather.7.cloned.1.call-done = bf16[2048,2816]{1,0:T(8,128)(2,1)} async-done(((bf16[64,2816]{1,0:T(8,128)(2,1)}), bf16[2048,2816]{1,0:T(8,128)(2,1)}) %all-gather.7.cloned.1.call-update) | async-done | bytes 11534352 | tf_op jit(solution)/shard_map/all_gather | solution.py:84
  104.9 6.3 fusion.83
  136.8 9.1 multiply_exponential_fusion
  157.2 5.8 slice.557
  250.9 6.2 slice.613
  257.1 5.9 slice.614
  324.3 9.6 pad.228
  333.9 9.3 pad.229
  345.9 9.4 pad.212
  355.3 9.3 pad.213
  383.9 13.4 multiply_convert_fusion.2
  397.3 6.6 multiply_reduce_fusion.7
  405.5 40.2 %all-gather.13.cloned.1.call-done = bf16[2048,6144]{1,0:T(8,128)(2,1)} async-done(((bf16[64,6144]{1,0:T(8,128)(2,1)}), bf16[2048,6144]{1,0:T(8,128)(2,1)}) %all-gather.13.cloned.1.call-update) | async-done | bytes 25165840 | tf_op jit(solution)/shard_map/all_gather | solution.py:122
  445.7 14.2 fusion.108
  460.0 141.4 %all-gather.15.cloned.1.call-done = bf16[2048,6144]{1,0:T(8,128)(2,1)} async-done(((bf16[64,6144]{1,0:T(8,128)(2,1)}), bf16[2048,6144]{1,0:T(8,128)(2,1)}) %all-gather.15.cloned.1.call-update) | async-done | bytes 25165840 | tf_op jit(solution)/shard_map/all_gather | solution.py:123
  601.3 14.3 fusion.109
  615.7 141.3 %all-gather.17.cloned.1.call-done = bf16[6144,2048]{1,0:T(8,128)(2,1)} async-done(((bf16[192,2048]{1,0:T(8,128)(2,1)}), bf16[6144,2048]{1,0:T(8,128)(2,1)}) %all-gather.17.cloned.1.call-update) | async-done | bytes 25165840 | tf_op jit(solution)/shard_map/all_gather | solution.py:124
  756.9 22.1 multiply_convert_fusion
  779.1 13.5 fusion.110
  792.6 15.7 multiply_reduce_fusion.5
  811.7 12.8 fusion.45
  824.5 7.4 convolution_convert_fusion.3
  835.8 5.8 slice.636
  841.6 5.7 slice.642
  847.3 5.7 slice.694
  853.0 11.9 slice.637
  864.9 11.9 slice.643
  876.7 11.9 slice.695
  900.0 11.9 slice.634
  911.9 11.9 slice.639
  950.4 9.5 convolution_convert_fusion.5
  1068.7 9.5 pad.261
  1091.5 9.4 pad.245
  1100.8 11.9 slice.697
  1119.4 9.4 pad.244
  1131.4 9.6 pad.260
  1143.4 8.1 collective-permute-done.4
  1152.9 7.1 collective-permute-done.5
  1168.2 23.0 rev.9
  1191.2 22.7 rev.8
  1213.9 8.5 multiply_reduce_fusion
  1223.2 5.7 convert_reduce_fusion.1
  1248.1 11.9 multiply_reduce_fusion.3
  1269.3 6.2 convolution_convert_fusion.4
  1276.7 13.7 convolution_convert_fusion.2
  1290.4 13.8 convolution_convert_fusion.1
  1305.5 14.0 convolution_convert_fusion
  1319.6 6.6 fusion.111
  1329.1 9.5 fusion.37
  1348.0 121.3 %reduce-scatter.17.cloned.1.call-done = bf16[512,2816]{1,0:T(8,128)(2,1)} async-done(((bf16[2048,2816]{1,0:T(8,128)(2,1)}), bf16[512,2816]{1,0:T(8,128)(2,1)}) %reduce-scatter.17.cloned.1.call-update) | async-done | bytes 2883600 | tf_op jit(solution)/shard_map/reduce_scatter | solution.py:45
  1473.9 413.0 %reduce-scatter.25.cloned.1.call-done = bf16[512,6144]{1,0:T(8,128)(2,1)} async-done(((bf16[2048,6144]{1,0:T(8,128)(2,1)}), bf16[512,6144]{1,0:T(8,128)(2,1)}) %reduce-scatter.25.cloned.1.call-update) | async-done | bytes 6291472 | tf_op jit(solution)/shard_map/reduce_scatter | solution.py:45
  1887.0 418.6 %reduce-scatter.29.cloned.1.call-done = bf16[512,6144]{1,0:T(8,128)(2,1)} async-done(((bf16[2048,6144]{1,0:T(8,128)(2,1)}), bf16[512,6144]{1,0:T(8,128)(2,1)}) %reduce-scatter.29.cloned.1.call-update) | async-done | bytes 6291472 | tf_op jit(solution)/shard_map/reduce_scatter | solution.py:45
  2305.7 418.4 %reduce-scatter.33.cloned.1.call-done = bf16[1536,2048]{1,0:T(8,128)(2,1)} async-done(((bf16[6144,2048]{1,0:T(8,128)(2,1)}), bf16[1536,2048]{1,0:T(8,128)(2,1)}) %reduce-scatter.33.cloned.1.call-update) | async-done | bytes 6291472 | tf_op jit(solution)/shard_map/reduce_scatter | solution.py:45
  2724.1 40.9 %all-reduce.79.cloned.1.call-done = (f32[2048]{0:T(1024)}, f32[4,2816]{1,0:T(4,128)}, f32[2816]{0:T(1024)}, f32[2816]{0:T(1024)}, f32[2816]{0:T(1024)}, /*index=5*/f32[2816]{0:T(1024)}, f32[2048]{0:T(1024)}) async-done(((f32[2048]{0:T(1024)}, f32[4,2816]{1,0:T(4,128)}, f32[2816]{0:T(1024)}, f32[2816]{0:T(1024)}, f32[2816]{0:T(1024)}, /*index=5*/f32[2816]{0:T(1024)}, f32[2048]{0:T(1024)}), (f32[2048]{0:T(1024)}, ...) | async-done | bytes 106512 | tf_op jit(solution)/shard_map/psum | solution.py:219
  2765.1 208.6 %all-reduce.81.cloned.1.call-done = (f32[16,176,176]{2,1,0:T(8,128)}, f32[16,176,176]{2,1,0:T(8,128)}) async-done(((f32[16,176,176]{2,1,0:T(8,128)}, f32[16,176,176]{2,1,0:T(8,128)}), (f32[16,176,176]{2,1,0:T(8,128)}, f32[16,176,176]{2,1,0:T(8,128)})) %all-reduce.81.cloned.1.call-update) | async-done | bytes 3964944 | tf_op jit(solution)/shard_map/psum | solution.py:219
  2973.8 14.6 fusion.35
  2990.3 31.1 reduce-scatter.39.cloned.1.call-done
  3023.7 46.3 %reduce-scatter.23.cloned.1.call-done = bf16[704,256]{1,0:T(8,128)(2,1)} async-done(((bf16[704,2048]{1,0:T(8,128)(2,1)}), bf16[704,256]{1,0:T(8,128)(2,1)}) %reduce-scatter.23.cloned.1.call-update) | async-done | bytes 360464 | tf_op jit(solution)/shard_map/reduce_scatter | solution.py:53
  3071.8 46.8 %reduce-scatter.37.cloned.1.call-done = bf16[352,512]{1,0:T(8,128)(2,1)} async-done(((bf16[2816,512]{1,0:T(8,128)(2,1)}), bf16[352,512]{1,0:T(8,128)(2,1)}) %reduce-scatter.37.cloned.1.call-update) | async-done | bytes 360464
  3120.9 63.1 %reduce-scatter.27.cloned.1.call-done = bf16[512,768]{1,0:T(8,128)(2,1)} async-done(((bf16[512,6144]{1,0:T(8,128)(2,1)}), bf16[512,768]{1,0:T(8,128)(2,1)}) %reduce-scatter.27.cloned.1.call-update) | async-done | bytes 786448 | tf_op jit(solution)/shard_map/reduce_scatter | solution.py:53
  3186.4 62.7 %reduce-scatter.31.cloned.1.call-done = bf16[512,768]{1,0:T(8,128)(2,1)} async-done(((bf16[512,6144]{1,0:T(8,128)(2,1)}), bf16[512,768]{1,0:T(8,128)(2,1)}) %reduce-scatter.31.cloned.1.call-update) | async-done | bytes 786448 | tf_op jit(solution)/shard_map/reduce_scatter | solution.py:53
  3251.6 63.0 %reduce-scatter.35.cloned.1.call-done = bf16[1536,256]{1,0:T(8,128)(2,1)} async-done(((bf16[1536,2048]{1,0:T(8,128)(2,1)}), bf16[1536,256]{1,0:T(8,128)(2,1)}) %reduce-scatter.35.cloned.1.call-update) | async-done | bytes 786448 | tf_op jit(solution)/shard_map/reduce_scatter | solution.py:53
  3317.0 55.0 %all-reduce.75.cloned.1.call-done = (f32[2048]{0:T(1024)}, f32[4,2816]{1,0:T(4,128)}, f32[2816]{0:T(1024)}, f32[2816]{0:T(1024)}, f32[2816]{0:T(1024)}, /*index=5*/f32[2816]{0:T(1024)}, f32[2048]{0:T(1024)}) async-done(((f32[2048]{0:T(1024)}, f32[4,2816]{1,0:T(4,128)}, f32[2816]{0:T(1024)}, f32[2816]{0:T(1024)}, f32[2816]{0:T(1024)}, /*index=5*/f32[2816]{0:T(1024)}, f32[2048]{0:T(1024)}), (f32[2048]{0:T(1024)}, ...) | async-done | bytes 106512 | tf_op jit(solution)/shard_map/psum | solution.py:218
  3372.0 102.9 %all-reduce.77.cloned.1.call-done = (f32[16,176,176]{2,1,0:T(8,128)}, f32[16,176,176]{2,1,0:T(8,128)}) async-done(((f32[16,176,176]{2,1,0:T(8,128)}, f32[16,176,176]{2,1,0:T(8,128)}), (f32[16,176,176]{2,1,0:T(8,128)}, f32[16,176,176]{2,1,0:T(8,128)})) %all-reduce.77.cloned.1.call-update) | async-done | bytes 3964944 | tf_op jit(solution)/shard_map/psum | solution.py:218
  (592 shorter events, 476.9 us)
Async XLA Ops:
  7.2 115.0 %copy-start = (bf16[16,176,176]{2,1,0:T(8,128)(2,1)S(1)}, bf16[16,176,176]{2,1,0:T(8,128)(2,1)}, u32[]{:S(2)}) copy-start(bf16[16,176,176]{2,1,0:T(8,128)(2,1)} %param.23) | copy-start | bytes 2973700
  7.2 97.7 %copy-start.41 = (f32[2048]{0:T(1024)S(1)}, f32[2048]{0:T(1024)}, u32[]{:S(2)}) copy-start(f32[2048]{0:T(1024)} %param.18) | copy-start | bytes 24580
  7.2 97.7 %all-gather.7.cloned.1.call-start = ((), (), s32[]{:S(2)}) async-start(), calls=%async_computation.12 | async-start | bytes 11894784 | tf_op jit(solution)/shard_map/all_gather | solution.py:84
  8.0 374.5 %all-gather.9.cloned.1.call-start = ((), (), s32[]{:S(2)}) async-start(), calls=%async_computation.13 | async-start | bytes 11894784 | tf_op jit(solution)/shard_map/all_gather | solution.py:85
  8.7 388.6 %all-gather.11.cloned.1.call-start = ((), (), s32[]{:S(2)}) async-start(), calls=%async_computation.14 | async-start | bytes 11894784 | tf_op jit(solution)/shard_map/all_gather | solution.py:86
  9.5 436.3 %all-gather.13.cloned.1.call-start = ((), (), s32[]{:S(2)}) async-start(), calls=%async_computation.15 | async-start | bytes 25952256 | tf_op jit(solution)/shard_map/all_gather | solution.py:122
  10.0 591.3 %all-gather.15.cloned.1.call-start = ((), (), s32[]{:S(2)}) async-start(), calls=%async_computation.16 | async-start | bytes 25952256 | tf_op jit(solution)/shard_map/all_gather | solution.py:123
  10.6 746.3 %all-gather.17.cloned.1.call-start = ((), (), s32[]{:S(2)}) async-start(), calls=%async_computation.17 | async-start | bytes 25952256 | tf_op jit(solution)/shard_map/all_gather | solution.py:124
  11.2 1331.5 %reduce-scatter.19.cloned.1.call-start = ((), (), s32[]{:S(2)}) async-start(), calls=%async_computation.19 | async-start | bytes 14417920 | tf_op jit(solution)/shard_map/reduce_scatter | solution.py:45
  11.5 99.7 %copy-start.112 = (f32[256]{0:T(256)}, f32[256]{0:T(256)S(1)}, u32[]{:S(2)}) copy-start(f32[256]{0:T(256)S(1)} %fusion.41) | copy-start | bytes 3076
  11.6 125.2 %copy-start.44 = (f32[2816]{0:T(1024)}, f32[2816]{0:T(1024)S(1)}, u32[]{:S(2)}) copy-start(f32[2816]{0:T(1024)S(1)} %broadcast_multiply_fusion) | copy-start | bytes 33796
  11.6 102.9 %copy-start.97 = (f32[4,2816]{1,0:T(4,128)S(1)}, f32[4,2816]{1,0:T(4,128)}, u32[]{:S(2)}) copy-start(f32[4,2816]{1,0:T(4,128)} %param.21) | copy-start | bytes 135172
  11.6 105.1 %copy-start.108 = (f32[2816]{0:T(1024)S(1)}, f32[2816]{0:T(1024)}, u32[]{:S(2)}) copy-start(f32[2816]{0:T(1024)} %param.22) | copy-start | bytes 33796
  111.3 5.5 collective-permute-start
  250.9 15.2 copy-start.66
  250.9 15.2 copy-start.67
  250.9 15.2 copy-start.68
  250.9 15.2 copy-start.69
  250.9 15.3 copy-start.46
  250.9 15.7 copy-start.54
  250.9 15.7 copy-start.55
  366.6 5.7 collective-permute-start.1
  372.3 5.8 collective-permute-start.2
  378.1 5.8 collective-permute-start.3
  405.5 195.9 %copy-start.14 = (bf16[256,2048]{1,0:T(8,128)(2,1)}, bf16[256,2048]{1,0:T(8,128)(2,1)S(1)}, u32[]{:S(2)}) copy-start(bf16[256,2048]{1,0:T(8,128)(2,1)S(1)} %multiply_convert_fusion.3) | copy-start | bytes 3145732
  792.6 15.7 copy-start.116
  831.9 515.5 %reduce-scatter.21.cloned.1.call-start = ((), (), s32[]{:S(2)}) async-start(), calls=%async_computation.20 | async-start | bytes 14417920 | tf_op jit(solution)/shard_map/reduce_scatter | solution.py:45
  959.9 509.4 %reduce-scatter.17.cloned.1.call-start = ((), (), s32[]{:S(2)}) async-start(), calls=%async_computation.18 | async-start | bytes 14417920 | tf_op jit(solution)/shard_map/reduce_scatter | solution.py:45
  1006.2 17.3 copy-start.70
  1006.2 17.3 copy-start.71
  1006.3 17.3 copy-start.72
  1006.3 17.3 copy-start.73
  1006.3 17.4 copy-start.47
  1009.8 14.3 copy-start.57
  1009.8 14.4 copy-start.96
  1009.8 14.5 copy-start.95
  1131.4 29.9 copy-start.75
  1142.1 9.4 collective-permute-start.4
  1151.6 8.4 collective-permute-start.5
  1160.0 53.9 %collective-permute-start.6 = (f32[2816]{0:T(1024)S(1)}, f32[2816]{0:T(1024)S(1)}, u32[]{:S(2)}, u32[]{:S(2)}) collective-permute-start(f32[2816]{0:T(1024)S(1)} %multiply_add_fusion.17), channel_id=1, source_target_pairs={{1,0},{2,1},{3,2},{5,4},{6,5},{7,6},{9,8},{10,9},{11,10},{13,12},{... | collective-permute-start | bytes 33800 | tf_op jit(solution)/shard_map/ppermute | solution.py:12
  1191.2 22.7 copy-start.45
  1191.2 22.7 copy-start.49
  1191.2 22.7 copy-start.51
  1248.1 18.3 copy-start.59
  1248.1 18.3 copy-start.61
  1248.1 18.3 copy-start.63
  1248.1 18.3 copy-start.65
  1260.0 6.3 collective-permute-start.7
  1275.5 611.5 %reduce-scatter.25.cloned.1.call-start = ((), (), s32[]{:S(2)}) async-start(), calls=%async_computation.22 | async-start | bytes 31457280 | tf_op jit(solution)/shard_map/reduce_scatter | solution.py:45
  1290.4 1015.3 %reduce-scatter.29.cloned.1.call-start = ((), (), s32[]{:S(2)}) async-start(), calls=%async_computation.24 | async-start | bytes 31457280 | tf_op jit(solution)/shard_map/reduce_scatter | solution.py:45
  1304.3 1419.8 %reduce-scatter.33.cloned.1.call-start = ((), (), s32[]{:S(2)}) async-start(), calls=%async_computation.26 | async-start | bytes 31457280 | tf_op jit(solution)/shard_map/reduce_scatter | solution.py:45
  1319.5 1445.5 %all-reduce.79.cloned.1.call-start = ((), (), s32[]{:S(2)}) async-start(), calls=%async_computation.32 | async-start | bytes 221184 | tf_op jit(solution)/shard_map/psum | solution.py:219
  1338.6 1635.1 %all-reduce.81.cloned.1.call-start = ((), (), s32[]{:S(2)}) async-start(), calls=%async_computation.33 | async-start | bytes 11534336 | tf_op jit(solution)/shard_map/psum | solution.py:219
  1342.7 1678.7 %reduce-scatter.39.cloned.1.call-start = ((), (), s32[]{:S(2)}) async-start(), calls=%async_computation.29 | async-start | bytes 3244032
  1347.3 1722.6 %reduce-scatter.23.cloned.1.call-start = ((), (), s32[]{:S(2)}) async-start(), calls=%async_computation.21 | async-start | bytes 3244032 | tf_op jit(solution)/shard_map/reduce_scatter | solution.py:53
  1347.9 1770.7 %reduce-scatter.37.cloned.1.call-start = ((), (), s32[]{:S(2)}) async-start(), calls=%async_computation.28 | async-start | bytes 3244032
  1473.8 1710.2 %reduce-scatter.27.cloned.1.call-start = ((), (), s32[]{:S(2)}) async-start(), calls=%async_computation.23 | async-start | bytes 7077888 | tf_op jit(solution)/shard_map/reduce_scatter | solution.py:53
  1886.9 1362.2 %reduce-scatter.31.cloned.1.call-start = ((), (), s32[]{:S(2)}) async-start(), calls=%async_computation.25 | async-start | bytes 7077888 | tf_op jit(solution)/shard_map/reduce_scatter | solution.py:53
  2305.6 1008.9 %reduce-scatter.35.cloned.1.call-start = ((), (), s32[]{:S(2)}) async-start(), calls=%async_computation.27 | async-start | bytes 7077888 | tf_op jit(solution)/shard_map/reduce_scatter | solution.py:53
  2724.1 647.9 %all-reduce.75.cloned.1.call-start = ((), (), s32[]{:S(2)}) async-start(), calls=%async_computation.30 | async-start | bytes 221184 | tf_op jit(solution)/shard_map/psum | solution.py:218
  2765.1 709.9 %all-reduce.77.cloned.1.call-start = ((), (), s32[]{:S(2)}) async-start(), calls=%async_computation.31 | async-start | bytes 11534336 | tf_op jit(solution)/shard_map/psum | solution.py:218
  2973.7 14.6 copy-start.113
  2973.7 14.6 copy-start.8
  2973.8 14.6 copy-start.40
  (83 other events, 475.1 us)
Sparse Core Ops, SparseCore 0:
  10.9 93.9 all-gather.6
  107.7 89.6 all-gather.8
  200.2 89.6 all-gather.10
  292.7 153.0 all-gather.12
  448.5 152.8 all-gather.14
  604.1 152.8 all-gather.16
  832.1 193.0 reduce-scatter.18
  1027.5 196.7 reduce-scatter.20
  1275.6 193.6 reduce-scatter.16
  1471.5 415.3 reduce-scatter.24
  1889.4 416.1 reduce-scatter.28
  2307.8 416.1 reduce-scatter.32
  2728.3 36.6 all-reduce.78
  2767.3 206.3 all-reduce.80
  2977.5 43.8 reduce-scatter.38
  3025.0 44.8 reduce-scatter.22
  3073.7 44.8 reduce-scatter.36
  3122.3 61.7 reduce-scatter.26
  3187.4 61.7 reduce-scatter.30
  3252.8 61.7 reduce-scatter.34
  3318.5 53.4 all-reduce.74
  3375.7 99.1 all-reduce.76
